TPU v7x, 32 devices: a whole 2x2x4 slice. The times are simulated.
32 devices in a mesh: station: 8 (over y, x, core), tm: 4 (over z).
Axes of the slice: x: 2, y: 2, z: 4, core: 2. Of those that a mesh axis runs over, the one named last changes fastest.
Arguments:
- samples: bfloat16 [64, 256, 2048], P('tm', 'station'), may hold values from -6 to 6
- history: bfloat16 [15, 256, 2048], P(None, 'station'), may hold values from -6 to 6
- taps: float32 [16, 2048], replicated, may hold values from -0.03125 to 0.03125
Outputs:
- visibility: float32 [1024, 2, 256, 256], P(('station', 'tm'))
- beam_power: float32 [64, 1024], P('tm', 'station')
All inputs are finite; a program needn't handle non-finite values.
Results may differ from a plain program's by a relative error of at most 0.0095.
Values may be sent and summed in bfloat16 or wider, within the bound.
A program may use at most 128 MiB of HBM per device.

v0:
```python
import math
import jax
import jax.numpy as jnp
from jax import lax
from jax.sharding import PartitionSpec as P


def passed_along(block, axis, distance):
    devices = range(lax.axis_size(axis))
    route = [(i - distance, i) for i in devices if i - distance in devices]
    return lax.ppermute(block, axis, route)


def dft_parts(frame_len, channels):
    sample_index = jnp.arange(frame_len, dtype=jnp.int32)
    channel_index = jnp.arange(channels, dtype=jnp.int32)
    phases = sample_index[:, None] * channel_index[None, :] % frame_len
    angles = phases.astype(jnp.float32) * (2.0 * math.pi / frame_len)
    return (jnp.cos(angles).astype(jnp.bfloat16), (-jnp.sin(angles)).astype(jnp.bfloat16))


def filter_frames(extended, taps, frames_out):
    span_taps = taps.shape[0]
    running = jnp.zeros((frames_out,) + extended.shape[1:], jnp.float32)
    for tap_index in range(span_taps):
        offset = span_taps - 1 - tap_index
        running = running + taps[tap_index][None, None, :] * extended[
            offset : offset + frames_out
        ].astype(jnp.float32)
    return jnp.swapaxes(running, 0, 1).astype(jnp.bfloat16)


def power_of(grouped):
    values = grouped.astype(jnp.float32)
    return jnp.sum(values * values, axis=(-3, -2)) * (1.0 / grouped.shape[-3])


def flat_pair(piece):
    chan_count, input_count, pair_count, frame_count = piece.shape
    flat = piece.reshape(chan_count, input_count, pair_count * frame_count)
    rotated = jnp.concatenate([-piece[:, :, 1:2], piece[:, :, 0:1]], axis=2)
    return (flat, rotated.reshape(chan_count, input_count, pair_count * frame_count))


def correlate(piece, norm_scale):
    flat, rotated = flat_pair(piece)
    real_part = (
        jnp.einsum("cak,cbk->cab", flat, flat, preferred_element_type=jnp.float32) * norm_scale
    )
    imag_part = (
        jnp.einsum("cak,cbk->cab", rotated, flat, preferred_element_type=jnp.float32) * norm_scale
    )
    return (real_part, imag_part)


def body(samples, history, taps):
    frames_dev = samples.shape[0]
    frame_len = samples.shape[2]
    span_taps = taps.shape[0]
    cos_part, sin_part = dft_parts(frame_len, frame_len // 2)
    tail_block = samples[frames_dev - (span_taps - 1) :]
    prior_frames = passed_along(tail_block, "tm", 1)
    prior_frames = jnp.where(lax.axis_index("tm") == 0, history, prior_frames)
    extended = jnp.concatenate([prior_frames, samples], axis=0)
    weighted = filter_frames(extended, taps, frames_dev)
    real_spec = jnp.einsum("nc,atn->cat", cos_part, weighted, preferred_element_type=jnp.float32)
    imag_spec = jnp.einsum("nc,atn->cat", sin_part, weighted, preferred_element_type=jnp.float32)
    spectra = jnp.stack([real_spec, imag_spec], axis=2).astype(jnp.bfloat16)
    time_groups = lax.axis_size("tm")
    norm_scale = 1.0 / (frames_dev * time_groups)
    gathered = lax.all_to_all(
        lax.all_to_all(spectra[None], "station", split_axis=1, concat_axis=2, tiled=True),
        "tm",
        split_axis=1,
        concat_axis=0,
        tiled=True,
    )
    own_channels = gathered.shape[1]
    inputs = gathered.shape[2]
    power_own = power_of(gathered)
    power_back = lax.all_to_all(power_own, "tm", split_axis=0, concat_axis=1, tiled=True)
    power_rows = jnp.transpose(power_back[0])

    def accumulate(block_index, running):
        time_piece = lax.dynamic_index_in_dim(gathered, block_index, 0, keepdims=False)
        real_part, imag_part = correlate(time_piece, norm_scale)
        partial_value = jnp.stack([real_part, imag_part], axis=1).astype(jnp.bfloat16)
        partial_value = lax.optimization_barrier(partial_value)
        return running + partial_value.astype(jnp.float32)

    initial_sum = jnp.zeros((own_channels, 2, inputs, inputs), jnp.float32)
    visibility = lax.fori_loop(0, time_groups, accumulate, initial_sum)
    return (visibility, power_rows)


def solution(mesh):
    return jax.shard_map(
        body,
        mesh=mesh,
        in_specs=(P("tm", "station", None), P(None, "station", None), P()),
        out_specs=(P(("station", "tm"), None, None, None), P("tm", "station")),
        check_vma=False,
    )
```

profile of v0, /device:TPU:0, one launch (start us, length us, event | category | flops | bytes accessed | tf_op | source)
XLA Modules:
  0.0 371.6 jit_solution(146463902237839219)
XLA Ops:
  0.6 3.2 slice.112
  3.8 6.2 %collective-permute-start = (bf16[15,32,2048]{2,1,0:T(8,128)(2,1)}, bf16[15,32,2048]{2,1,0:T(8,128)(2,1)}, u32[]{:S(2)}, u32[]{:S(2)}) collective-permute-start(bf16[15,32,2048]{2,1,0:T(8,128)(2,1)} %slice.112), channel_id=1, source_target_pairs={{0,1},{1,2},{2,3},{4,5},{5,6},{6,7},{8,9},{9,10},{10,11},{12,13},{... | collective-permute-start | bytes 5898248 | tf_op jit(solution)/shard_map/ppermute | solution.py:11
  10.1 1.6 fusion.60
  11.7 39.5 %collective-permute-done = bf16[15,32,2048]{2,1,0:T(8,128)(2,1)} collective-permute-done((bf16[15,32,2048]{2,1,0:T(8,128)(2,1)}, bf16[15,32,2048]{2,1,0:T(8,128)(2,1)}, u32[]{:S(2)}, u32[]{:S(2)}) %collective-permute-start) | collective-permute-done | bytes 1966112 | tf_op jit(solution)/shard_map/ppermute | solution.py:11
  51.1 1.8 broadcast_select_fusion
  52.9 9.5 %add_convert_fusion = bf16[16,32,2048]{2,1,0:T(8,128)(2,1)S(1)} fusion(bf16[16,32,2048]{2,1,0:T(8,128)(2,1)S(1)} %copy-done, bf16[15,32,2048]{2,1,0:T(8,128)(2,1)S(1)} %broadcast_select_fusion, f32[2048]{0:T(1024)S(1)} %bitcast.116, f32[2048]{0:T(1024)S(1)} %bitcast.117, f32[2048]{0:T(1024)S(1)} %bitcast.103, f32[2048]{0:T(1024)S(1)} %bitcast.104, ...), kind=kLoop, calls=%fused_computation.53 | loop fusion | flops 66060288 | bytes 6291456 | tf_op jit(solution)/shard_map/convert_element_type | solution.py:30
  62.4 31.8 %fusion.42 = bf16[1,1024,32,1,16]{1,2,4,3,0:T(8,128)(2,1)S(1)} fusion(bf16[16,32,2048]{2,1,0:T(8,128)(2,1)S(1)} %add_convert_fusion), kind=kOutput, calls=%fused_computation.75 | convolution fusion | flops 2179465216 | bytes 3145728 | tf_op jit(solution)/shard_map/nc,atn->cat/dot_general | solution.py:66
  94.2 32.5 %fusion.47 = bf16[1,1024,32,1,16]{1,2,4,3,0:T(8,128)(2,1)S(1)} fusion(bf16[16,32,2048]{2,1,0:T(8,128)(2,1)S(1)} %add_convert_fusion), kind=kOutput, calls=%fused_computation.76 | convolution fusion | flops 2181562368 | bytes 3145728 | tf_op jit(solution)/shard_map/nc,atn->cat/dot_general | solution.py:67
  126.8 12.1 %copy.33 = bf16[1,1024,32,2,16]{2,4,3,0,1:T(8,128)(2,1)} copy(bf16[1,1024,32,2,16]{1,2,4,3,0:T(8,128)(2,1)S(1)} %pad_maximum_fusion.3) | data formatting | bytes 4194304 | tf_op jit(solution)/shard_map/stack | solution.py:68
  138.9 10.1 %reshape.82 = bf16[8,2,65536]{2,1,0:T(2,128)(2,1)S(1)} reshape(bf16[1024,1,2,16,32]{4,3,2,1,0:T(8,128)(2,1)} %bitcast.96) | data formatting | bytes 4194304
  149.1 30.2 %all_to_all.39 = bf16[8,2,65536]{2,1,0:T(2,128)(2,1)} all-to-all(bf16[8,2,65536]{2,1,0:T(2,128)(2,1)S(1)} %reshape.82), channel_id=1, replica_groups=mesh['station'=8,'tm'=4] {'station'}, dimensions={0} | all-to-all | bytes 4194304 | tf_op jit(solution)/shard_map/all_to_all | solution.py:72
  179.3 8.6 %reshape.83 = bf16[1024,1,2,16,32]{4,3,2,1,0:T(8,128)(2,1)} reshape(bf16[8,2,65536]{2,1,0:T(2,128)(2,1)} %all_to_all.39) | data formatting | bytes 4194304
  187.9 9.3 %copy.42 = bf16[1,8,128,32,2,16]{2,1,5,4,3,0:T(8,128)(2,1)S(1)} copy(bf16[1,8,128,32,2,16]{3,5,4,2,1,0:T(8,128)(2,1)} %bitcast.97) | data formatting | bytes 4194304 | tf_op jit(solution)/shard_map/all_to_all | solution.py:72
  197.2 1.7 copy.35
  198.9 4.9 %copy.36 = bf16[1,128,256,2,16]{2,4,3,0,1:T(8,128)(2,1)} copy(bf16[1,128,256,2,16]{1,4,3,2,0:T(8,128)(2,1)} %bitcast.99) | data formatting | bytes 4194304 | tf_op jit(solution)/shard_map/all_to_all | solution.py:72
  203.8 5.8 %all-to-all-start.1 = ((bf16[1,128,256,2,16]{2,4,3,0,1:T(8,128)(2,1)}), bf16[1,128,256,2,16]{2,4,3,0,1:T(8,128)(2,1)S(1)}, u32[]{:S(2)}, u32[]{:S(2)}) async-start(bf16[1,128,256,2,16]{2,4,3,0,1:T(8,128)(2,1)} %copy.36), calls=%async_computation.1 | async-start | bytes 4194304 | tf_op jit(solution)/shard_map/all_to_all | solution.py:71
  209.6 47.5 %all-to-all-done.1 = bf16[1,128,256,2,16]{2,4,3,0,1:T(8,128)(2,1)S(1)} async-done(((bf16[1,128,256,2,16]{2,4,3,0,1:T(8,128)(2,1)}), bf16[1,128,256,2,16]{2,4,3,0,1:T(8,128)(2,1)S(1)}, u32[]{:S(2)}, u32[]{:S(2)}) %all-to-all-start.1) | async-done | bytes 2097184 | tf_op jit(solution)/shard_map/all_to_all | solution.py:71
  258.4 3.2 all-to-all-start.2
  261.7 96.2 %while.14 = (s32[]{:T(128)}, f32[32,2,256,256]{3,2,0,1:T(8,128)}, bf16[4,32,256,2,16]{2,4,3,1,0:T(8,128)(2,1)S(1)}, s32[]{:T(128)}, s32[]{:T(128)}) while((s32[]{:T(128)}, f32[32,2,256,256]{3,2,0,1:T(8,128)}, bf16[4,32,256,2,16]{2,4,3,1,0:T(8,128)(2,1)S(1)}, s32[]{:T(128)}, s32[]{:T(128)}) %tuple.65), condition=%wide.region_1.2_spmd.clone, body=%wide.region_0.1_spmd.clone.sunk | while | flops 293994496 | bytes 72876112 | solution.py:92
  263.2 3.2 fusion.79
  266.4 6.3 %pad_maximum_fusion.7 = bf16[32,2,256,256]{3,2,0,1:T(8,128)(2,1)} fusion(bf16[32,1,256,256]{3,2,0,1:T(8,128)(2,1)S(1)} %fusion.78, bf16[32,1,256,256]{3,2,0,1:T(8,128)(2,1)} %fusion.79), kind=kLoop, calls=%fused_computation.1.clone.1 | loop fusion | flops 4194304 | bytes 16777216 | tf_op jit(solution)/shard_map/while/body/eval_jaxpr/stack | solution.py:87
  272.8 9.9 %select_add_fusion.2 = f32[32,2,256,256]{3,2,0,1:T(8,128)} fusion(f32[32,2,256,256]{3,2,0,1:T(8,128)} %get-tuple-element.149, bf16[32,2,256,256]{3,2,0,1:T(8,128)(2,1)} %pad_maximum_fusion.7, pred[]{:T(512)S(6)} %compare.4), kind=kLoop, calls=%fused_computation.clone.1 | loop fusion | flops 12582912 | bytes 41943040 | tf_op jit(solution)/shard_map/while/body/eval_jaxpr/add | solution.py:89
  284.2 3.2 fusion.79
  287.5 6.3 %pad_maximum_fusion.7 = bf16[32,2,256,256]{3,2,0,1:T(8,128)(2,1)} fusion(bf16[32,1,256,256]{3,2,0,1:T(8,128)(2,1)S(1)} %fusion.78, bf16[32,1,256,256]{3,2,0,1:T(8,128)(2,1)} %fusion.79), kind=kLoop, calls=%fused_computation.1.clone.1 | loop fusion | flops 4194304 | bytes 16777216 | tf_op jit(solution)/shard_map/while/body/eval_jaxpr/stack | solution.py:87
  293.8 14.0 %select_add_fusion.2 = f32[32,2,256,256]{3,2,0,1:T(8,128)} fusion(f32[32,2,256,256]{3,2,0,1:T(8,128)} %get-tuple-element.149, bf16[32,2,256,256]{3,2,0,1:T(8,128)(2,1)} %pad_maximum_fusion.7, pred[]{:T(512)S(6)} %compare.4), kind=kLoop, calls=%fused_computation.clone.1 | loop fusion | flops 12582912 | bytes 41943040 | tf_op jit(solution)/shard_map/while/body/eval_jaxpr/add | solution.py:89
  309.3 3.2 fusion.79
  312.5 6.3 %pad_maximum_fusion.7 = bf16[32,2,256,256]{3,2,0,1:T(8,128)(2,1)} fusion(bf16[32,1,256,256]{3,2,0,1:T(8,128)(2,1)S(1)} %fusion.78, bf16[32,1,256,256]{3,2,0,1:T(8,128)(2,1)} %fusion.79), kind=kLoop, calls=%fused_computation.1.clone.1 | loop fusion | flops 4194304 | bytes 16777216 | tf_op jit(solution)/shard_map/while/body/eval_jaxpr/stack | solution.py:87
  318.9 14.0 %select_add_fusion.2 = f32[32,2,256,256]{3,2,0,1:T(8,128)} fusion(f32[32,2,256,256]{3,2,0,1:T(8,128)} %get-tuple-element.149, bf16[32,2,256,256]{3,2,0,1:T(8,128)(2,1)} %pad_maximum_fusion.7, pred[]{:T(512)S(6)} %compare.4), kind=kLoop, calls=%fused_computation.clone.1 | loop fusion | flops 12582912 | bytes 41943040 | tf_op jit(solution)/shard_map/while/body/eval_jaxpr/add | solution.py:89
  334.3 3.2 fusion.79
  337.6 6.3 %pad_maximum_fusion.7 = bf16[32,2,256,256]{3,2,0,1:T(8,128)(2,1)} fusion(bf16[32,1,256,256]{3,2,0,1:T(8,128)(2,1)S(1)} %fusion.78, bf16[32,1,256,256]{3,2,0,1:T(8,128)(2,1)} %fusion.79), kind=kLoop, calls=%fused_computation.1.clone.1 | loop fusion | flops 4194304 | bytes 16777216 | tf_op jit(solution)/shard_map/while/body/eval_jaxpr/stack | solution.py:87
  343.9 14.0 %select_add_fusion.2 = f32[32,2,256,256]{3,2,0,1:T(8,128)} fusion(f32[32,2,256,256]{3,2,0,1:T(8,128)} %get-tuple-element.149, bf16[32,2,256,256]{3,2,0,1:T(8,128)(2,1)} %pad_maximum_fusion.7, pred[]{:T(512)S(6)} %compare.4), kind=kLoop, calls=%fused_computation.clone.1 | loop fusion | flops 12582912 | bytes 41943040 | tf_op jit(solution)/shard_map/while/body/eval_jaxpr/add | solution.py:89
  357.9 11.7 %copy.41 = f32[32,2,256,256]{3,2,1,0:T(8,128)} copy(f32[32,2,256,256]{3,2,0,1:T(8,128)} %get-tuple-element.94) | data formatting | bytes 33554432
  (36 shorter events, 9.3 us)
Async XLA Ops:
  0.6 52.3 %copy-start = (bf16[16,32,2048]{2,1,0:T(8,128)(2,1)S(1)}, bf16[16,32,2048]{2,1,0:T(8,128)(2,1)}, u32[]{:S(2)}) copy-start(bf16[16,32,2048]{2,1,0:T(8,128)(2,1)} %param.5) | copy-start | bytes 6291460
  3.8 47.3 %collective-permute-start = (bf16[15,32,2048]{2,1,0:T(8,128)(2,1)}, bf16[15,32,2048]{2,1,0:T(8,128)(2,1)}, u32[]{:S(2)}, u32[]{:S(2)}) collective-permute-start(bf16[15,32,2048]{2,1,0:T(8,128)(2,1)} %slice.112), channel_id=1, source_target_pairs={{0,1},{1,2},{2,3},{4,5},{5,6},{6,7},{8,9},{9,10},{10,11},{12,13},{... | collective-permute-start | bytes 5898248 | tf_op jit(solution)/shard_map/ppermute | solution.py:11
  203.8 53.3 %all-to-all-start.1 = ((bf16[1,128,256,2,16]{2,4,3,0,1:T(8,128)(2,1)}), bf16[1,128,256,2,16]{2,4,3,0,1:T(8,128)(2,1)S(1)}, u32[]{:S(2)}, u32[]{:S(2)}) async-start(bf16[1,128,256,2,16]{2,4,3,0,1:T(8,128)(2,1)} %copy.36), calls=%async_computation.1 | async-start | bytes 4194304 | tf_op jit(solution)/shard_map/all_to_all | solution.py:71
  258.4 111.2 %all-to-all-start.2 = ((f32[4,1,512]{2,1,0:T(1,128)}), f32[4,1,512]{2,1,0:T(1,128)S(1)}, u32[]{:S(2)}, u32[]{:S(2)}) async-start(f32[4,1,512]{2,1,0:T(1,128)} %reshape.84), calls=%async_computation.2 | async-start | bytes 16384 | tf_op jit(solution)/shard_map/all_to_all | solution.py:81
where the time goes:
time: 373 us; the launch traced here: 372 us
  other arithmetic  90.2 us (24%)
  waiting for transfers between devices  87 us (23%)
  matrix products  82.4 us (22%)
  local copies, waits for them, and re-layouts  65.6 us (18%)
  blocking collectives  30.2 us (8%)
  starting transfers between devices  15.2 us (4%)
    add x4, other arithmetic, accumulate(): return running + partial_value.astype(jnp.float32)  51.9 us
    all_to_all x1, waiting for transfers between devices, body(): lax.all_to_all(lax.all_to_all(spectra[None], 'station', split_axis=1, con...  47.5 us
    ppermute x1, waiting for transfers between devices, passed_along(): return lax.ppermute(block, axis, route)  39.5 us
    dot_general x1, matrix products, body(): jnp.einsum('nc,atn->cat', sin_part, weighted, preferred_element_type=jnp....  32.5 us
    dot_general x1, matrix products, body(): jnp.einsum('nc,atn->cat', cos_part, weighted, preferred_element_type=jnp....  31.8 us
    unnamed x7, local copies, waits for them, and re-layouts  31.2 us
    all_to_all x1, blocking collectives, body(): lax.all_to_all(spectra[None], 'station', split_axis=1, concat_axis=2, til...  30.2 us
    another operation x4, other arithmetic, accumulate(): jnp.stack([real_part, imag_part], axis=1).astype(jnp.bfloat16)  25.4 us
  transfers between devices with their start and end apart: 3, of which 2 were waited for; matrix products, arithmetic and copies ran while one was open for 29% of the time, Pallas kernels for 0%

commit v1 on v0

--- a/solution.py
+++ b/solution.py
@@ -1,8 +1,29 @@
+import functools
 import math
 import jax
 import jax.numpy as jnp
 from jax import lax
 from jax.sharding import PartitionSpec as P
+
+
+def connect_the_lanes(x_part, mesh_ax, d_out, on_dim):
+    even = lax.axis_size(mesh_ax)
+    d_next, upper = (even, lax.axis_index(mesh_ax))
+    out_arr = x_part.shape[d_out] // d_next
+    earlier = list(x_part.shape)
+    earlier[d_out] = out_arr
+    outer = earlier[on_dim]
+    earlier[on_dim] = outer * d_next
+    b_now = jnp.zeros(earlier, x_part.dtype)
+    for c in range(d_next):
+        s_next = lax.dynamic_slice_in_dim(x_part, (upper ^ c) * out_arr, out_arr, axis=d_out)
+        if c:
+            s_next = lax.ppermute(s_next, mesh_ax, [(i0, i0 ^ c) for i0 in range(d_next)])
+        b_now = lax.dynamic_update_slice_in_dim(b_now, s_next, (upper ^ c) * outer, axis=on_dim)
+    return b_now
+
+
+group_numbers = functools.partial(connect_the_lanes, mesh_ax="station", d_out=1, on_dim=2)
 
 
 def passed_along(block, axis, distance):
@@ -69,11 +90,7 @@
     time_groups = lax.axis_size("tm")
     norm_scale = 1.0 / (frames_dev * time_groups)
     gathered = lax.all_to_all(
-        lax.all_to_all(spectra[None], "station", split_axis=1, concat_axis=2, tiled=True),
-        "tm",
-        split_axis=1,
-        concat_axis=0,
-        tiled=True,
+        group_numbers(spectra[None]), "tm", split_axis=1, concat_axis=0, tiled=True
     )
     own_channels = gathered.shape[1]
     inputs = gathered.shape[2]

time: 373 us -> 624 us (1.67); the launches traced: 372 us -> 615 us
  local copies, waits for them, and re-layouts: 65.6 us -> 328 us
  blocking collectives: 30.2 us -> 0 us
  starting transfers between devices: 15.2 us -> 22.7 us
    dynamic_update_slice x0 -> x8, local copies, waits for them, and re-layouts: none -> 289 us  [connect_the_lanes(): lax.dynamic_update_slice_in_dim(b_now, s_next, (upper ^ c) * outer, axis=...]
    all_to_all x1 -> x0, blocking collectives: 30.2 us -> none  [body(): lax.all_to_all(spectra[None], 'station', split_axis=1, concat_axis=2, til...]
    unnamed x7 -> x5, local copies, waits for them, and re-layouts: 31.2 us -> 12.4 us
    all_to_all x3 -> x0, local copies, waits for them, and re-layouts: 15.9 us -> none  [body(): lax.all_to_all(spectra[None], 'station', split_axis=1, concat_axis=2, til...]
    ppermute x0 -> x7, local copies, waits for them, and re-layouts: none -> 13.4 us  [connect_the_lanes(): lax.ppermute(s_next, mesh_ax, [(i0, i0 ^ c) for i0 in range(d_next)])]
    another operation x1 -> x7, local copies, waits for them, and re-layouts: 12.1 us -> 3.55 us  [body(): spectra = jnp.stack([real_spec, imag_spec], axis=2).astype(jnp.bfloat16)]
    ppermute x0 -> x7, starting transfers between devices: none -> 7.47 us  [connect_the_lanes(): lax.ppermute(s_next, mesh_ax, [(i0, i0 ^ c) for i0 in range(d_next)])]
  transfers between devices with their start and end apart: 3 -> 10, of which waited for: 2 -> 3; matrix products, arithmetic and copies ran while one was open for 29% -> 61% of each run, Pallas kernels for 0% -> 0%
where the time goes in v1:
time: 624 us; the launch traced here: 615 us
  local copies, waits for them, and re-layouts  328 us (53%)
  other arithmetic  90.5 us (15%)
  waiting for transfers between devices  90.2 us (14%)
  matrix products  82.7 us (13%)
  starting transfers between devices  22.7 us (4%)
    dynamic_update_slice x8, local copies, waits for them, and re-layouts, connect_the_lanes(): lax.dynamic_update_slice_in_dim(b_now, s_next, (upper ^ c) * outer, axis=...  289 us
    add x4, other arithmetic, accumulate(): return running + partial_value.astype(jnp.float32)  51.8 us
    all_to_all x1, waiting for transfers between devices, body(): lax.all_to_all(group_numbers(spectra[None]), 'tm', split_axis=1, concat_a...  49.5 us
    ppermute x1, waiting for transfers between devices, passed_along(): return lax.ppermute(block, axis, route)  39.5 us
    dot_general x1, matrix products, body(): jnp.einsum('nc,atn->cat', sin_part, weighted, preferred_element_type=jnp....  32.8 us
    dot_general x1, matrix products, body(): jnp.einsum('nc,atn->cat', cos_part, weighted, preferred_element_type=jnp....  31.8 us
    another operation x4, other arithmetic, accumulate(): jnp.stack([real_part, imag_part], axis=1).astype(jnp.bfloat16)  25.4 us
    ppermute x7, local copies, waits for them, and re-layouts, connect_the_lanes(): lax.ppermute(s_next, mesh_ax, [(i0, i0 ^ c) for i0 in range(d_next)])  13.4 us
  transfers between devices with their start and end apart: 10, of which 3 were waited for; matrix products, arithmetic and copies ran while one was open for 61% of the time, Pallas kernels for 0%

profile of v1, /device:TPU:0, one launch (start us, length us, event | category | flops | bytes accessed | tf_op | source)
XLA Modules:
  0.0 615.0 jit_solution(16801796142537030364)
XLA Ops:
  0.6 3.2 slice.112
  3.8 6.2 %collective-permute-start = (bf16[15,32,2048]{2,1,0:T(8,128)(2,1)}, bf16[15,32,2048]{2,1,0:T(8,128)(2,1)}, u32[]{:S(2)}, u32[]{:S(2)}) collective-permute-start(bf16[15,32,2048]{2,1,0:T(8,128)(2,1)} %slice.112), channel_id=1, source_target_pairs={{0,1},{1,2},{2,3},{4,5},{5,6},{6,7},{8,9},{9,10},{10,11},{12,13},{... | collective-permute-start | bytes 5898248 | tf_op jit(solution)/shard_map/ppermute | solution.py:32
  11.7 39.5 %collective-permute-done = bf16[15,32,2048]{2,1,0:T(8,128)(2,1)} collective-permute-done((bf16[15,32,2048]{2,1,0:T(8,128)(2,1)}, bf16[15,32,2048]{2,1,0:T(8,128)(2,1)}, u32[]{:S(2)}, u32[]{:S(2)}) %collective-permute-start) | collective-permute-done | bytes 1966112 | tf_op jit(solution)/shard_map/ppermute | solution.py:32
  52.9 9.5 %add_convert_fusion = bf16[16,32,2048]{2,1,0:T(8,128)(2,1)S(1)} fusion(bf16[16,32,2048]{2,1,0:T(8,128)(2,1)S(1)} %copy-done, bf16[15,32,2048]{2,1,0:T(8,128)(2,1)S(1)} %broadcast_select_fusion, f32[2048]{0:T(1024)S(1)} %bitcast.133, f32[2048]{0:T(1024)S(1)} %bitcast.134, f32[2048]{0:T(1024)S(1)} %bitcast.120, f32[2048]{0:T(1024)S(1)} %bitcast.121, ...), kind=kLoop, calls=%fused_computation.53 | loop fusion | flops 66060288 | bytes 6291456 | tf_op jit(solution)/shard_map/convert_element_type | solution.py:51
  62.4 31.8 %fusion.42 = bf16[1024,32,1,16]{0,1,3,2:T(8,128)(2,1)S(1)} fusion(bf16[16,32,2048]{2,1,0:T(8,128)(2,1)S(1)} %add_convert_fusion), kind=kOutput, calls=%fused_computation.90 | convolution fusion | flops 2179465216 | bytes 3145728 | tf_op jit(solution)/shard_map/nc,atn->cat/dot_general | solution.py:87
  94.2 32.8 %fusion.47 = bf16[1024,32,1,16]{0,1,3,2:T(8,128)(2,1)S(1)} fusion(bf16[16,32,2048]{2,1,0:T(8,128)(2,1)S(1)} %add_convert_fusion), kind=kOutput, calls=%fused_computation.91 | convolution fusion | flops 2181562368 | bytes 3145728 | tf_op jit(solution)/shard_map/nc,atn->cat/dot_general | solution.py:88
  142.8 12.8 %dynamic_update_slice.24 = bf16[1,128,256,2,16]{2,4,3,0,1:T(8,128)(2,1)} dynamic-update-slice(bf16[1,128,256,2,16]{2,4,3,0,1:T(8,128)(2,1)} %broadcast_in_dim.10, bf16[1,128,32,2,16]{2,4,3,0,1:T(8,128)(2,1)S(1)} %copy.81, s32[]{:T(128)} %constant.65.clone.1, s32[]{:T(128)} %constant.65.clone.1, s32[]{:T(128)S(6)} %select_n.75, s32[]{:T(128)} %constant.65.clone.1, s32[]{:T(128)} %constant.65.clone.1) | dynamic-update-slice | bytes 524292 | tf_op jit(solution)/shard_map/dynamic_update_slice | solution.py:22
  157.2 44.3 %dynamic_update_slice.25 = bf16[1,128,256,2,16]{2,4,3,0,1:T(8,128)(2,1)} dynamic-update-slice(bf16[1,128,256,2,16]{2,4,3,0,1:T(8,128)(2,1)} %dynamic_update_slice.24, bf16[1,128,32,2,16]{2,4,3,0,1:T(8,128)(2,1)S(1)} %copy.83, s32[]{:T(128)} %constant.65.clone.1, s32[]{:T(128)} %constant.65.clone.1, s32[]{:T(128)S(6)} %select_n.77, s32[]{:T(128)} %constant.65.clone.1, s32[]{:T(128)} %constant.65.clone.1) | dynamic-update-slice | bytes 524292 | tf_op jit(solution)/shard_map/dynamic_update_slice | solution.py:22
  204.2 44.3 %dynamic_update_slice.26 = bf16[1,128,256,2,16]{2,4,3,0,1:T(8,128)(2,1)} dynamic-update-slice(bf16[1,128,256,2,16]{2,4,3,0,1:T(8,128)(2,1)} %dynamic_update_slice.25, bf16[1,128,32,2,16]{2,4,3,0,1:T(8,128)(2,1)S(1)} %copy.85, s32[]{:T(128)} %constant.65.clone.1, s32[]{:T(128)} %constant.65.clone.1, s32[]{:T(128)S(6)} %select_n.79, s32[]{:T(128)} %constant.65.clone.1, s32[]{:T(128)} %constant.65.clone.1) | dynamic-update-slice | bytes 524292 | tf_op jit(solution)/shard_map/dynamic_update_slice | solution.py:22
  248.5 2.7 copy.87
  251.2 44.3 %dynamic_update_slice.27 = bf16[1,128,256,2,16]{2,4,3,0,1:T(8,128)(2,1)} dynamic-update-slice(bf16[1,128,256,2,16]{2,4,3,0,1:T(8,128)(2,1)} %dynamic_update_slice.26, bf16[1,128,32,2,16]{2,4,3,0,1:T(8,128)(2,1)S(1)} %copy.87, s32[]{:T(128)} %constant.65.clone.1, s32[]{:T(128)} %constant.65.clone.1, s32[]{:T(128)S(6)} %select_n.81, s32[]{:T(128)} %constant.65.clone.1, s32[]{:T(128)} %constant.65.clone.1) | dynamic-update-slice | bytes 524292 | tf_op jit(solution)/shard_map/dynamic_update_slice | solution.py:22
  297.1 12.0 %dynamic_update_slice.28 = bf16[1,128,256,2,16]{2,4,3,0,1:T(8,128)(2,1)} dynamic-update-slice(bf16[1,128,256,2,16]{2,4,3,0,1:T(8,128)(2,1)} %dynamic_update_slice.27, bf16[1,128,32,2,16]{2,4,3,0,1:T(8,128)(2,1)S(1)} %copy.89, s32[]{:T(128)} %constant.65.clone.1, s32[]{:T(128)} %constant.65.clone.1, s32[]{:T(128)S(6)} %select_n.83, s32[]{:T(128)} %constant.65.clone.1, s32[]{:T(128)} %constant.65.clone.1) | dynamic-update-slice | bytes 524292 | tf_op jit(solution)/shard_map/dynamic_update_slice | solution.py:22
  310.7 43.9 %dynamic_update_slice.29 = bf16[1,128,256,2,16]{2,4,3,0,1:T(8,128)(2,1)} dynamic-update-slice(bf16[1,128,256,2,16]{2,4,3,0,1:T(8,128)(2,1)} %dynamic_update_slice.28, bf16[1,128,32,2,16]{2,4,3,0,1:T(8,128)(2,1)S(1)} %copy.91, s32[]{:T(128)} %constant.65.clone.1, s32[]{:T(128)} %constant.65.clone.1, s32[]{:T(128)S(6)} %select_n.85, s32[]{:T(128)} %constant.65.clone.1, s32[]{:T(128)} %constant.65.clone.1) | dynamic-update-slice | bytes 524292 | tf_op jit(solution)/shard_map/dynamic_update_slice | solution.py:22
  356.2 43.6 %dynamic_update_slice.30 = bf16[1,128,256,2,16]{2,4,3,0,1:T(8,128)(2,1)} dynamic-update-slice(bf16[1,128,256,2,16]{2,4,3,0,1:T(8,128)(2,1)} %dynamic_update_slice.29, bf16[1,128,32,2,16]{2,4,3,0,1:T(8,128)(2,1)S(1)} %copy.93, s32[]{:T(128)} %constant.65.clone.1, s32[]{:T(128)} %constant.65.clone.1, s32[]{:T(128)S(6)} %select_n.87, s32[]{:T(128)} %constant.65.clone.1, s32[]{:T(128)} %constant.65.clone.1) | dynamic-update-slice | bytes 524292 | tf_op jit(solution)/shard_map/dynamic_update_slice | solution.py:22
  401.5 43.6 %dynamic_update_slice.31 = bf16[1,128,256,2,16]{2,4,3,0,1:T(8,128)(2,1)} dynamic-update-slice(bf16[1,128,256,2,16]{2,4,3,0,1:T(8,128)(2,1)} %dynamic_update_slice.30, bf16[1,128,32,2,16]{2,4,3,0,1:T(8,128)(2,1)S(1)} %copy.95, s32[]{:T(128)} %constant.65.clone.1, s32[]{:T(128)} %constant.65.clone.1, s32[]{:T(128)S(6)} %select_n.89, s32[]{:T(128)} %constant.65.clone.1, s32[]{:T(128)} %constant.65.clone.1) | dynamic-update-slice | bytes 524292 | tf_op jit(solution)/shard_map/dynamic_update_slice | solution.py:22
  445.1 5.8 all-to-all-start
  450.9 49.5 %all-to-all-done = bf16[1,128,256,2,16]{2,4,3,0,1:T(8,128)(2,1)S(1)} async-done(((bf16[1,128,256,2,16]{2,4,3,0,1:T(8,128)(2,1)}), bf16[1,128,256,2,16]{2,4,3,0,1:T(8,128)(2,1)S(1)}, u32[]{:S(2)}, u32[]{:S(2)}) %all-to-all-start) | async-done | bytes 2097184 | tf_op jit(solution)/shard_map/all_to_all | solution.py:92
  501.7 3.2 all-to-all-start.1
  505.0 96.2 %while.14 = (s32[]{:T(128)}, f32[32,2,256,256]{3,2,0,1:T(8,128)}, bf16[4,32,256,2,16]{2,4,3,1,0:T(8,128)(2,1)S(1)}, s32[]{:T(128)}, s32[]{:T(128)}) while((s32[]{:T(128)}, f32[32,2,256,256]{3,2,0,1:T(8,128)}, bf16[4,32,256,2,16]{2,4,3,1,0:T(8,128)(2,1)S(1)}, s32[]{:T(128)}, s32[]{:T(128)}) %tuple.69), condition=%wide.region_1.2_spmd.clone, body=%wide.region_0.1_spmd.clone.sunk | while | flops 293994496 | bytes 72876112 | solution.py:109
  506.5 3.2 fusion.88
  509.8 6.3 %pad_maximum_fusion.6 = bf16[32,2,256,256]{3,2,0,1:T(8,128)(2,1)} fusion(bf16[32,1,256,256]{3,2,0,1:T(8,128)(2,1)S(1)} %fusion.87, bf16[32,1,256,256]{3,2,0,1:T(8,128)(2,1)} %fusion.88), kind=kLoop, calls=%fused_computation.1.clone.1 | loop fusion | flops 4194304 | bytes 16777216 | tf_op jit(solution)/shard_map/while/body/eval_jaxpr/stack | solution.py:104
  516.1 9.9 %select_add_fusion.2 = f32[32,2,256,256]{3,2,0,1:T(8,128)} fusion(f32[32,2,256,256]{3,2,0,1:T(8,128)} %get-tuple-element.152, bf16[32,2,256,256]{3,2,0,1:T(8,128)(2,1)} %pad_maximum_fusion.6, pred[]{:T(512)S(6)} %compare.4), kind=kLoop, calls=%fused_computation.clone.1 | loop fusion | flops 12582912 | bytes 41943040 | tf_op jit(solution)/shard_map/while/body/eval_jaxpr/add | solution.py:106
  527.5 3.2 fusion.88
  530.8 6.3 %pad_maximum_fusion.6 = bf16[32,2,256,256]{3,2,0,1:T(8,128)(2,1)} fusion(bf16[32,1,256,256]{3,2,0,1:T(8,128)(2,1)S(1)} %fusion.87, bf16[32,1,256,256]{3,2,0,1:T(8,128)(2,1)} %fusion.88), kind=kLoop, calls=%fused_computation.1.clone.1 | loop fusion | flops 4194304 | bytes 16777216 | tf_op jit(solution)/shard_map/while/body/eval_jaxpr/stack | solution.py:104
  537.1 14.0 %select_add_fusion.2 = f32[32,2,256,256]{3,2,0,1:T(8,128)} fusion(f32[32,2,256,256]{3,2,0,1:T(8,128)} %get-tuple-element.152, bf16[32,2,256,256]{3,2,0,1:T(8,128)(2,1)} %pad_maximum_fusion.6, pred[]{:T(512)S(6)} %compare.4), kind=kLoop, calls=%fused_computation.clone.1 | loop fusion | flops 12582912 | bytes 41943040 | tf_op jit(solution)/shard_map/while/body/eval_jaxpr/add | solution.py:106
  552.6 3.2 fusion.88
  555.8 6.3 %pad_maximum_fusion.6 = bf16[32,2,256,256]{3,2,0,1:T(8,128)(2,1)} fusion(bf16[32,1,256,256]{3,2,0,1:T(8,128)(2,1)S(1)} %fusion.87, bf16[32,1,256,256]{3,2,0,1:T(8,128)(2,1)} %fusion.88), kind=kLoop, calls=%fused_computation.1.clone.1 | loop fusion | flops 4194304 | bytes 16777216 | tf_op jit(solution)/shard_map/while/body/eval_jaxpr/stack | solution.py:104
  562.2 14.0 %select_add_fusion.2 = f32[32,2,256,256]{3,2,0,1:T(8,128)} fusion(f32[32,2,256,256]{3,2,0,1:T(8,128)} %get-tuple-element.152, bf16[32,2,256,256]{3,2,0,1:T(8,128)(2,1)} %pad_maximum_fusion.6, pred[]{:T(512)S(6)} %compare.4), kind=kLoop, calls=%fused_computation.clone.1 | loop fusion | flops 12582912 | bytes 41943040 | tf_op jit(solution)/shard_map/while/body/eval_jaxpr/add | solution.py:106
  577.6 3.2 fusion.88
  580.9 6.3 %pad_maximum_fusion.6 = bf16[32,2,256,256]{3,2,0,1:T(8,128)(2,1)} fusion(bf16[32,1,256,256]{3,2,0,1:T(8,128)(2,1)S(1)} %fusion.87, bf16[32,1,256,256]{3,2,0,1:T(8,128)(2,1)} %fusion.88), kind=kLoop, calls=%fused_computation.1.clone.1 | loop fusion | flops 4194304 | bytes 16777216 | tf_op jit(solution)/shard_map/while/body/eval_jaxpr/stack | solution.py:104
  587.2 14.0 %select_add_fusion.2 = f32[32,2,256,256]{3,2,0,1:T(8,128)} fusion(f32[32,2,256,256]{3,2,0,1:T(8,128)} %get-tuple-element.152, bf16[32,2,256,256]{3,2,0,1:T(8,128)(2,1)} %pad_maximum_fusion.6, pred[]{:T(512)S(6)} %compare.4), kind=kLoop, calls=%fused_computation.clone.1 | loop fusion | flops 12582912 | bytes 41943040 | tf_op jit(solution)/shard_map/while/body/eval_jaxpr/add | solution.py:106
  601.2 11.7 %copy.99 = f32[32,2,256,256]{3,2,1,0:T(8,128)} copy(f32[32,2,256,256]{3,2,0,1:T(8,128)} %get-tuple-element.89) | data formatting | bytes 33554432
  (68 shorter events, 39.1 us)
Async XLA Ops:
  0.6 52.3 %copy-start = (bf16[16,32,2048]{2,1,0:T(8,128)(2,1)S(1)}, bf16[16,32,2048]{2,1,0:T(8,128)(2,1)}, u32[]{:S(2)}) copy-start(bf16[16,32,2048]{2,1,0:T(8,128)(2,1)} %param.5) | copy-start | bytes 6291460
  3.8 47.3 %collective-permute-start = (bf16[15,32,2048]{2,1,0:T(8,128)(2,1)}, bf16[15,32,2048]{2,1,0:T(8,128)(2,1)}, u32[]{:S(2)}, u32[]{:S(2)}) collective-permute-start(bf16[15,32,2048]{2,1,0:T(8,128)(2,1)} %slice.112), channel_id=1, source_target_pairs={{0,1},{1,2},{2,3},{4,5},{5,6},{6,7},{8,9},{9,10},{10,11},{12,13},{... | collective-permute-start | bytes 5898248 | tf_op jit(solution)/shard_map/ppermute | solution.py:32
  128.2 6.5 %collective-permute-start.1 = (bf16[1,128,32,2,16]{1,4,3,2,0:T(8,128)(2,1)}, bf16[1,128,32,2,16]{1,4,3,2,0:T(8,128)(2,1)S(1)}, u32[]{:S(2)}, u32[]{:S(2)}) collective-permute-start(bf16[1,128,32,2,16]{1,4,3,2,0:T(8,128)(2,1)} %bitcast.90), channel_id=1, source_target_pairs={{0,4},{4,0},{8,12},{12,8},{16,20},{20,16},{24,28},{28,24},{1,5},{5... | collective-permute-start | bytes 786440 | tf_op jit(solution)/shard_map/ppermute | solution.py:21
  129.0 9.4 %collective-permute-start.2 = (bf16[1,128,32,2,16]{1,4,3,2,0:T(8,128)(2,1)}, bf16[1,128,32,2,16]{1,4,3,2,0:T(8,128)(2,1)}, u32[]{:S(2)}, u32[]{:S(2)}) collective-permute-start(bf16[1,128,32,2,16]{1,4,3,2,0:T(8,128)(2,1)} %bitcast.89), channel_id=1, source_target_pairs={{0,8},{4,12},{8,0},{12,4},{16,24},{20,28},{24,16},{28,20},{1,9},{5... | collective-permute-start | bytes 786440 | tf_op jit(solution)/shard_map/ppermute | solution.py:21
  131.3 117.2 %collective-permute-start.3 = (bf16[1,128,32,2,16]{1,4,3,2,0:T(8,128)(2,1)}, bf16[1,128,32,2,16]{1,4,3,2,0:T(8,128)(2,1)}, u32[]{:S(2)}, u32[]{:S(2)}) collective-permute-start(bf16[1,128,32,2,16]{1,4,3,2,0:T(8,128)(2,1)} %bitcast.88), channel_id=1, source_target_pairs={{0,12},{4,8},{8,4},{12,0},{16,28},{20,24},{24,20},{28,16},{1,13},{... | collective-permute-start | bytes 786440 | tf_op jit(solution)/shard_map/ppermute | solution.py:21
  132.5 163.0 %collective-permute-start.4 = (bf16[1,128,32,2,16]{1,4,3,2,0:T(8,128)(2,1)}, bf16[1,128,32,2,16]{1,4,3,2,0:T(8,128)(2,1)S(1)}, u32[]{:S(2)}, u32[]{:S(2)}) collective-permute-start(bf16[1,128,32,2,16]{1,4,3,2,0:T(8,128)(2,1)} %bitcast.87), channel_id=1, source_target_pairs={{0,16},{4,20},{8,24},{12,28},{16,0},{20,4},{24,8},{28,12},{1,17},{... | collective-permute-start | bytes 786440 | tf_op jit(solution)/shard_map/ppermute | solution.py:21
  134.2 174.9 %collective-permute-start.5 = (bf16[1,128,32,2,16]{1,4,3,2,0:T(8,128)(2,1)S(1)}, bf16[1,128,32,2,16]{1,4,3,2,0:T(8,128)(2,1)S(1)}, u32[]{:S(2)}, u32[]{:S(2)}) collective-permute-start(bf16[1,128,32,2,16]{1,4,3,2,0:T(8,128)(2,1)S(1)} %bitcast.116), channel_id=1, source_target_pairs={{0,20},{4,16},{8,28},{12,24},{16,4},{20,0},{24,12},{28,8},{1,21},{... | collective-permute-start | bytes 786440 | tf_op jit(solution)/shard_map/ppermute | solution.py:21
  134.6 219.9 %collective-permute-start.6 = (bf16[1,128,32,2,16]{1,4,3,2,0:T(8,128)(2,1)S(1)}, bf16[1,128,32,2,16]{1,4,3,2,0:T(8,128)(2,1)S(1)}, u32[]{:S(2)}, u32[]{:S(2)}) collective-permute-start(bf16[1,128,32,2,16]{1,4,3,2,0:T(8,128)(2,1)S(1)} %bitcast.115), channel_id=1, source_target_pairs={{0,24},{4,28},{8,16},{12,20},{16,8},{20,12},{24,0},{28,4},{1,25},{... | collective-permute-start | bytes 786440 | tf_op jit(solution)/shard_map/ppermute | solution.py:21
  138.4 261.4 %collective-permute-start.7 = (bf16[1,128,32,2,16]{1,4,3,2,0:T(8,128)(2,1)S(1)}, bf16[1,128,32,2,16]{1,4,3,2,0:T(8,128)(2,1)S(1)}, u32[]{:S(2)}, u32[]{:S(2)}) collective-permute-start(bf16[1,128,32,2,16]{1,4,3,2,0:T(8,128)(2,1)S(1)} %bitcast.114), channel_id=1, source_target_pairs={{0,28},{4,24},{8,20},{12,16},{16,12},{20,8},{24,4},{28,0},{1,29},{... | collective-permute-start | bytes 786440 | tf_op jit(solution)/shard_map/ppermute | solution.py:21
  445.1 55.3 %all-to-all-start = ((bf16[1,128,256,2,16]{2,4,3,0,1:T(8,128)(2,1)}), bf16[1,128,256,2,16]{2,4,3,0,1:T(8,128)(2,1)S(1)}, u32[]{:S(2)}, u32[]{:S(2)}) async-start(bf16[1,128,256,2,16]{2,4,3,0,1:T(8,128)(2,1)} %dynamic_update_slice.31), calls=%async_computation | async-start | bytes 4194304 | tf_op jit(solution)/shard_map/all_to_all | solution.py:92
  501.7 111.1 %all-to-all-start.1 = ((f32[4,1,512]{2,1,0:T(1,128)}), f32[4,1,512]{2,1,0:T(1,128)S(1)}, u32[]{:S(2)}, u32[]{:S(2)}) async-start(f32[4,1,512]{2,1,0:T(1,128)} %reshape.57), calls=%async_computation.1 | async-start | bytes 16384 | tf_op jit(solution)/shard_map/all_to_all | solution.py:98
